TPU v7x, 512 devices: a whole 4x4x16 slice. The times are simulated.
512 devices in a mesh: blk: 64 (over x_hi, z, core), tgt: 8 (over y, x_lo).
Axes of the slice: x: 4 (x_hi: 2, x_lo: 2; x = x_hi * 2 + x_lo), y: 4, z: 16, core: 2. Of those that a mesh axis runs over, the one named last changes fastest.
Arguments:
- queries: bfloat16 [65536, 1024], P(('blk', 'tgt')), may hold values from -6 to 6
- keys: bfloat16 [4096, 1024], P('blk'), may hold values from -6 to 6
- values: bfloat16 [4096, 1024], P('blk'), may hold values from -6 to 6
- out_weight: bfloat16 [1024, 1024], P('tgt'), may hold values from -0.1875 to 0.1875
- out_grad: bfloat16 [65536, 1024], P(('blk', 'tgt')), may hold values from -24 to 24
Outputs:
- outputs: bfloat16 [65536, 1024], P(('blk', 'tgt'))
- query_grad: bfloat16 [65536, 1024], P(('blk', 'tgt'))
- key_grad: bfloat16 [4096, 1024], P('blk', 'tgt')
- value_grad: bfloat16 [4096, 1024], P('blk', 'tgt')
- weight_grad: bfloat16 [1024, 1024], P('tgt', 'blk')
All inputs are finite; a program needn't handle non-finite values.
Results may differ from a plain program's by a relative error of at most 0.017.
Values may be sent and summed in bfloat16 or wider, within the bound.
No kernel may reach another device: no remote copies, remote signals or barrier semaphores. Data moves between devices by JAX's collectives and lax.ppermute only.
A program may use at most 64 MiB of HBM per device.

v0:
```python
import jax
import jax.numpy as jnp
from jax import lax
from jax.sharding import PartitionSpec as P

D = 1024
HEADS = 16
HD = 64
WIN = 5
SRC_DEV = 64


def shifted(value, axis, steps):
    count = lax.axis_size(axis)
    pairs = [(source, (source + steps) % count) for source in range(count)]
    return lax.ppermute(value, axis, pairs)


def for_sending(value):
    return jax.tree.map(lambda a: a.astype(jnp.bfloat16) if a.dtype == jnp.float32 else a, value)


def head_block(query_cols, key_cols, value_cols, grad_cols, group_heads):
    scale = HD ** (-0.5)
    count = query_cols.shape[0]
    width = key_cols.shape[0]
    query_heads = query_cols.reshape(count, group_heads, HD)
    key_heads = key_cols.reshape(width, group_heads, HD)
    value_heads = value_cols.reshape(width, group_heads, HD)
    grad_heads = grad_cols.reshape(count, group_heads, HD)
    scores = (
        jnp.einsum("rhd,jhd->hrj", query_heads, key_heads, preferred_element_type=jnp.float32)
        * scale
    )
    top = jnp.max(scores, axis=-1, keepdims=True)
    expo = jnp.exp(scores - top)
    probs = expo / jnp.sum(expo, axis=-1, keepdims=True)
    probs_low = probs.astype(jnp.bfloat16)
    attended = jnp.einsum(
        "hrj,jhd->rhd", probs_low, value_heads, preferred_element_type=jnp.float32
    )
    attended = attended.reshape(count, group_heads * HD).astype(jnp.bfloat16)
    prob_grad = jnp.einsum(
        "rhd,jhd->hrj", grad_heads, value_heads, preferred_element_type=jnp.float32
    )
    center = jnp.sum(probs * prob_grad, axis=-1, keepdims=True)
    score_grad = (scale * probs * (prob_grad - center)).astype(jnp.bfloat16)
    query_grad = jnp.einsum(
        "hrj,jhd->rhd", score_grad, key_heads, preferred_element_type=jnp.float32
    )
    query_grad = query_grad.reshape(count, group_heads * HD).astype(jnp.bfloat16)
    key_part = jnp.einsum(
        "hrj,rhd->jhd", score_grad, query_heads, preferred_element_type=jnp.float32
    )
    value_part = jnp.einsum(
        "hrj,rhd->jhd", probs_low, grad_heads, preferred_element_type=jnp.float32
    )
    return (
        attended,
        query_grad,
        key_part.reshape(width, group_heads * HD),
        value_part.reshape(width, group_heads * HD),
    )


def local(queries, keys, values, out_weight, out_grad):
    full_weight = lax.all_gather(out_weight, "tgt", axis=0, tiled=True)
    current = (keys, values)
    key_list = [keys]
    value_list = [values]
    for step in range(1, WIN):
        current = shifted((current[0], current[1]), "blk", 1)
        key_list.append(current[0])
        value_list.append(current[1])
    seen_keys = jnp.concatenate(key_list, axis=0)
    seen_values = jnp.concatenate(value_list, axis=0)
    attended_grad = jnp.dot(out_grad, full_weight.T, preferred_element_type=jnp.float32).astype(
        jnp.bfloat16
    )
    group_heads = min(4, HEADS)
    span = group_heads * HD
    pieces = []
    for first in range(0, D, span):
        pieces.append(
            head_block(
                queries[:, first : first + span],
                seen_keys[:, first : first + span],
                seen_values[:, first : first + span],
                attended_grad[:, first : first + span],
                group_heads,
            )
        )
    attended = jnp.concatenate([p[0] for p in pieces], axis=1)
    query_grad = jnp.concatenate([p[1] for p in pieces], axis=1)
    key_part = jnp.concatenate([p[2] for p in pieces], axis=1)
    value_part = jnp.concatenate([p[3] for p in pieces], axis=1)
    outputs = jnp.dot(attended, full_weight, preferred_element_type=jnp.float32).astype(
        jnp.bfloat16
    )
    rows = SRC_DEV
    carried = (key_part[(WIN - 1) * rows : WIN * rows], value_part[(WIN - 1) * rows : WIN * rows])
    for step in range(WIN - 2, -1, -1):
        moved = shifted((for_sending(carried[0]), for_sending(carried[1])), "blk", -1)
        carried = (
            moved[0] + key_part[step * rows : (step + 1) * rows],
            moved[1] + value_part[step * rows : (step + 1) * rows],
        )
    key_total, value_total = carried
    key_grad, value_grad = (
        lax.psum_scatter(
            key_total.astype(jnp.bfloat16), "tgt", scatter_dimension=1, tiled=True
        ).astype(jnp.float32),
        lax.psum_scatter(
            value_total.astype(jnp.bfloat16), "tgt", scatter_dimension=1, tiled=True
        ).astype(jnp.float32),
    )
    tile_sum = lax.psum_scatter(
        jnp.einsum("rc,re->ce", attended, out_grad, preferred_element_type=jnp.float32).astype(
            jnp.bfloat16
        ),
        "tgt",
        scatter_dimension=0,
        tiled=True,
    ).astype(jnp.float32)
    weight_grad = lax.psum_scatter(tile_sum, "blk", scatter_dimension=1, tiled=True)
    return (
        outputs,
        query_grad,
        key_grad.astype(jnp.bfloat16),
        value_grad.astype(jnp.bfloat16),
        weight_grad.astype(jnp.bfloat16),
    )


def solution(mesh):
    return jax.shard_map(
        local,
        mesh=mesh,
        in_specs=(
            P(("blk", "tgt"), None),
            P("blk", None),
            P("blk", None),
            P("tgt", None),
            P(("blk", "tgt"), None),
        ),
        out_specs=(
            P(("blk", "tgt"), None),
            P(("blk", "tgt"), None),
            P("blk", "tgt"),
            P("blk", "tgt"),
            P("tgt", "blk"),
        ),
        check_vma=False,
    )
```

profile of v0, /device:TPU:8, one launch (start us, length us, event | category | flops | bytes accessed | tf_op | source)
XLA Modules:
  0.0 457.7 jit_solution(14117293037007560445)
XLA Ops:
  8.0 1.9 collective-permute-start.4
  9.9 3.9 collective-permute-start
  17.1 7.0 %collective-permute-done.4 = bf16[64,1024]{1,0:T(8,128)(2,1)S(1)} collective-permute-done((bf16[64,1024]{1,0:T(8,128)(2,1)}, bf16[64,1024]{1,0:T(8,128)(2,1)S(1)}, u32[]{:S(2)}, u32[]{:S(2)}) %collective-permute-start.4) | collective-permute-done | bytes 131104 | tf_op jit(solution)/shard_map/ppermute | solution.py:16
  24.1 1.9 collective-permute-start.5
  26.1 1.9 collective-permute-start.1
  28.0 6.0 %collective-permute-done.5 = bf16[64,1024]{1,0:T(8,128)(2,1)S(1)} collective-permute-done((bf16[64,1024]{1,0:T(8,128)(2,1)S(1)}, bf16[64,1024]{1,0:T(8,128)(2,1)S(1)}, u32[]{:S(2)}, u32[]{:S(2)}) %collective-permute-start.5) | collective-permute-done | bytes 131104 | tf_op jit(solution)/shard_map/ppermute | solution.py:16
  34.0 1.9 collective-permute-start.6
  38.0 6.0 %collective-permute-done.6 = bf16[64,1024]{1,0:T(8,128)(2,1)S(1)} collective-permute-done((bf16[64,1024]{1,0:T(8,128)(2,1)S(1)}, bf16[64,1024]{1,0:T(8,128)(2,1)S(1)}, u32[]{:S(2)}, u32[]{:S(2)}) %collective-permute-start.6) | collective-permute-done | bytes 131104 | tf_op jit(solution)/shard_map/ppermute | solution.py:16
  44.0 1.9 collective-permute-start.7
  48.0 6.0 %collective-permute-done.7 = bf16[64,1024]{1,0:T(8,128)(2,1)S(1)} collective-permute-done((bf16[64,1024]{1,0:T(8,128)(2,1)S(1)}, bf16[64,1024]{1,0:T(8,128)(2,1)S(1)}, u32[]{:S(2)}, u32[]{:S(2)}) %collective-permute-start.7) | collective-permute-done | bytes 131104 | tf_op jit(solution)/shard_map/ppermute | solution.py:16
  63.3 2.0 convolution_convert_fusion
  65.4 14.1 %all-gather.2.cloned.1.call-done = bf16[1024,1024]{1,0:T(8,128)(2,1)} async-done(((bf16[128,1024]{1,0:T(8,128)(2,1)}), bf16[1024,1024]{1,0:T(8,128)(2,1)}) %all-gather.2.cloned.1.call-update) | async-done | bytes 2097168 | tf_op jit(solution)/shard_map/all_gather | solution.py:67
  79.5 2.4 convolution_convert_fusion.1
  97.9 2.1 collective-permute-start.12
  104.3 1.9 collective-permute-start.8
  107.2 3.9 collective-permute-start.13
  111.2 5.1 %collective-permute-start.9 = (bf16[64,1024]{1,0:T(8,128)(2,1)S(1)}, bf16[64,1024]{1,0:T(8,128)(2,1)S(1)}, u32[]{:S(2)}, u32[]{:S(2)}) collective-permute-start(bf16[64,1024]{1,0:T(8,128)(2,1)S(1)} %fusion.23), channel_id=1, source_target_pairs={{0,504},{8,0},{16,8},{24,16},{32,24},{40,32},{48,40},{56,48},{64,5... | collective-permute-start | bytes 393224 | tf_op jit(solution)/shard_map/ppermute | solution.py:16
  116.3 4.8 %collective-permute-start.14 = (bf16[64,1024]{1,0:T(8,128)(2,1)S(1)}, bf16[64,1024]{1,0:T(8,128)(2,1)S(1)}, u32[]{:S(2)}, u32[]{:S(2)}) collective-permute-start(bf16[64,1024]{1,0:T(8,128)(2,1)S(1)} %fusion.18), channel_id=1, source_target_pairs={{0,504},{8,0},{16,8},{24,16},{32,24},{40,32},{48,40},{56,48},{64,5... | collective-permute-start | bytes 393224 | tf_op jit(solution)/shard_map/ppermute | solution.py:16
  121.2 5.1 %collective-permute-start.10 = (bf16[64,1024]{1,0:T(8,128)(2,1)S(1)}, bf16[64,1024]{1,0:T(8,128)(2,1)S(1)}, u32[]{:S(2)}, u32[]{:S(2)}) collective-permute-start(bf16[64,1024]{1,0:T(8,128)(2,1)S(1)} %fusion.22), channel_id=1, source_target_pairs={{0,504},{8,0},{16,8},{24,16},{32,24},{40,32},{48,40},{56,48},{64,5... | collective-permute-start | bytes 393224 | tf_op jit(solution)/shard_map/ppermute | solution.py:16
  126.3 4.8 %collective-permute-start.15 = (bf16[64,1024]{1,0:T(8,128)(2,1)S(1)}, bf16[64,1024]{1,0:T(8,128)(2,1)S(1)}, u32[]{:S(2)}, u32[]{:S(2)}) collective-permute-start(bf16[64,1024]{1,0:T(8,128)(2,1)S(1)} %fusion.17), channel_id=1, source_target_pairs={{0,504},{8,0},{16,8},{24,16},{32,24},{40,32},{48,40},{56,48},{64,5... | collective-permute-start | bytes 393224 | tf_op jit(solution)/shard_map/ppermute | solution.py:16
  131.9 5.1 %collective-permute-start.11 = (bf16[64,1024]{1,0:T(8,128)(2,1)}, bf16[64,1024]{1,0:T(8,128)(2,1)}, u32[]{:S(2)}, u32[]{:S(2)}) collective-permute-start(bf16[64,1024]{1,0:T(8,128)(2,1)} %fusion.21), channel_id=1, source_target_pairs={{0,504},{8,0},{16,8},{24,16},{32,24},{40,32},{48,40},{56,48},{64,5... | collective-permute-start | bytes 393224 | tf_op jit(solution)/shard_map/ppermute | solution.py:16
  151.1 35.5 %reduce-scatter.15.cloned.1.call-done = bf16[128,64]{1,0:T(8,128)(2,1)} async-done(((bf16[1024,64]{1,0:T(8,128)(2,1)}), bf16[128,64]{1,0:T(8,128)(2,1)}) %reduce-scatter.15.cloned.1.call-update) | async-done | bytes 16400
  188.0 45.3 %reduce-scatter.13.cloned.1.call-done = bf16[128,64]{1,0:T(8,128)(2,1)} async-done(((bf16[1024,64]{1,0:T(8,128)(2,1)}), bf16[128,64]{1,0:T(8,128)(2,1)}) %reduce-scatter.13.cloned.1.call-update) | async-done | bytes 16400
  234.8 214.9 %reduce-scatter.17.cloned.1.call-done = f32[16,128]{1,0:T(8,128)} async-done(((f32[1024,128]{1,0:T(8,128)}), f32[16,128]{1,0:T(8,128)}) %reduce-scatter.17.cloned.1.call-update) | async-done | bytes 8208
  (198 shorter events, 57.4 us)
Async XLA Ops:
  7.2 56.1 %copy-start = (bf16[128,1024]{1,0:T(8,128)(2,1)S(1)}, bf16[128,1024]{1,0:T(8,128)(2,1)}, u32[]{:S(2)}) copy-start(bf16[128,1024]{1,0:T(8,128)(2,1)} %param.9) | copy-start | bytes 786436
  7.2 72.3 %all-gather.2.cloned.1.call-start = ((), (), s32[]{:S(2)}) async-start(), calls=%async_computation.4 | async-start | bytes 2359296 | tf_op jit(solution)/shard_map/all_gather | solution.py:67
  7.9 136.6 %reduce-scatter.11.cloned.1.call-start = ((), (), s32[]{:S(2)}) async-start(), calls=%async_computation.5 | async-start | bytes 2359296 | tf_op jit(solution)/shard_map/reduce_scatter | solution.py:117
  8.0 16.2 %collective-permute-start.4 = (bf16[64,1024]{1,0:T(8,128)(2,1)}, bf16[64,1024]{1,0:T(8,128)(2,1)S(1)}, u32[]{:S(2)}, u32[]{:S(2)}) collective-permute-start(bf16[64,1024]{1,0:T(8,128)(2,1)} %param.6), channel_id=1, source_target_pairs={{0,8},{8,16},{16,24},{24,32},{32,40},{40,48},{48,56},{56,64},{64,7... | collective-permute-start | bytes 393224 | tf_op jit(solution)/shard_map/ppermute | solution.py:16
  9.9 16.2 %collective-permute-start = (bf16[64,1024]{1,0:T(8,128)(2,1)}, bf16[64,1024]{1,0:T(8,128)(2,1)S(1)}, u32[]{:S(2)}, u32[]{:S(2)}) collective-permute-start(bf16[64,1024]{1,0:T(8,128)(2,1)} %param.7), channel_id=1, source_target_pairs={{0,8},{8,16},{16,24},{24,32},{32,40},{40,48},{48,56},{56,64},{64,7... | collective-permute-start | bytes 393224 | tf_op jit(solution)/shard_map/ppermute | solution.py:16
  16.7 79.4 %copy-start.24 = (bf16[128,256]{0,1:T(8,128)(2,1)}, bf16[128,256]{0,1:T(8,128)(2,1)S(1)}, u32[]{:S(2)}) copy-start(bf16[128,256]{0,1:T(8,128)(2,1)S(1)} %copy.74) | copy-start | bytes 196612
  17.1 42.6 %copy-start.26 = (bf16[128,256]{0,1:T(8,128)(2,1)}, bf16[128,256]{0,1:T(8,128)(2,1)S(1)}, u32[]{:S(2)}) copy-start(bf16[128,256]{0,1:T(8,128)(2,1)S(1)} %copy.80) | copy-start | bytes 196612
  24.1 9.9 %collective-permute-start.5 = (bf16[64,1024]{1,0:T(8,128)(2,1)S(1)}, bf16[64,1024]{1,0:T(8,128)(2,1)S(1)}, u32[]{:S(2)}, u32[]{:S(2)}) collective-permute-start(bf16[64,1024]{1,0:T(8,128)(2,1)S(1)} %collective-permute-done.4), channel_id=1, source_target_pairs={{0,8},{8,16},{16,24},{24,32},{32,40},{40,48},{48,56},{56,64},{64,7... | collective-permute-start | bytes 393224 | tf_op jit(solution)/shard_map/ppermute | solution.py:16
  26.1 10.0 %collective-permute-start.1 = (bf16[64,1024]{1,0:T(8,128)(2,1)S(1)}, bf16[64,1024]{1,0:T(8,128)(2,1)S(1)}, u32[]{:S(2)}, u32[]{:S(2)}) collective-permute-start(bf16[64,1024]{1,0:T(8,128)(2,1)S(1)} %collective-permute-done), channel_id=1, source_target_pairs={{0,8},{8,16},{16,24},{24,32},{32,40},{40,48},{48,56},{56,64},{64,7... | collective-permute-start | bytes 393224 | tf_op jit(solution)/shard_map/ppermute | solution.py:16
  34.0 10.0 %collective-permute-start.6 = (bf16[64,1024]{1,0:T(8,128)(2,1)S(1)}, bf16[64,1024]{1,0:T(8,128)(2,1)S(1)}, u32[]{:S(2)}, u32[]{:S(2)}) collective-permute-start(bf16[64,1024]{1,0:T(8,128)(2,1)S(1)} %collective-permute-done.5), channel_id=1, source_target_pairs={{0,8},{8,16},{16,24},{24,32},{32,40},{40,48},{48,56},{56,64},{64,7... | collective-permute-start | bytes 393224 | tf_op jit(solution)/shard_map/ppermute | solution.py:16
  36.1 10.0 %collective-permute-start.2 = (bf16[64,1024]{1,0:T(8,128)(2,1)S(1)}, bf16[64,1024]{1,0:T(8,128)(2,1)S(1)}, u32[]{:S(2)}, u32[]{:S(2)}) collective-permute-start(bf16[64,1024]{1,0:T(8,128)(2,1)S(1)} %collective-permute-done.1), channel_id=1, source_target_pairs={{0,8},{8,16},{16,24},{24,32},{32,40},{40,48},{48,56},{56,64},{64,7... | collective-permute-start | bytes 393224 | tf_op jit(solution)/shard_map/ppermute | solution.py:16
  44.0 10.0 %collective-permute-start.7 = (bf16[64,1024]{1,0:T(8,128)(2,1)S(1)}, bf16[64,1024]{1,0:T(8,128)(2,1)S(1)}, u32[]{:S(2)}, u32[]{:S(2)}) collective-permute-start(bf16[64,1024]{1,0:T(8,128)(2,1)S(1)} %collective-permute-done.6), channel_id=1, source_target_pairs={{0,8},{8,16},{16,24},{24,32},{32,40},{40,48},{48,56},{56,64},{64,7... | collective-permute-start | bytes 393224 | tf_op jit(solution)/shard_map/ppermute | solution.py:16
  46.0 10.0 %collective-permute-start.3 = (bf16[64,1024]{1,0:T(8,128)(2,1)S(1)}, bf16[64,1024]{1,0:T(8,128)(2,1)S(1)}, u32[]{:S(2)}, u32[]{:S(2)}) collective-permute-start(bf16[64,1024]{1,0:T(8,128)(2,1)S(1)} %collective-permute-done.2), channel_id=1, source_target_pairs={{0,8},{8,16},{16,24},{24,32},{32,40},{40,48},{48,56},{56,64},{64,7... | collective-permute-start | bytes 393224 | tf_op jit(solution)/shard_map/ppermute | solution.py:16
  65.3 121.2 %reduce-scatter.15.cloned.1.call-start = ((), (), s32[]{:S(2)}) async-start(), calls=%async_computation.7 | async-start | bytes 294912
  97.9 8.3 %collective-permute-start.12 = (bf16[64,1024]{1,0:T(8,128)(2,1)}, bf16[64,1024]{1,0:T(8,128)(2,1)}, u32[]{:S(2)}, u32[]{:S(2)}) collective-permute-start(bf16[64,1024]{1,0:T(8,128)(2,1)} %slice.154), channel_id=1, source_target_pairs={{0,504},{8,0},{16,8},{24,16},{32,24},{40,32},{48,40},{56,48},{64,5... | collective-permute-start | bytes 393224 | tf_op jit(solution)/shard_map/ppermute | solution.py:16
  104.3 6.8 %collective-permute-start.8 = (bf16[64,1024]{1,0:T(8,128)(2,1)S(1)}, bf16[64,1024]{1,0:T(8,128)(2,1)S(1)}, u32[]{:S(2)}, u32[]{:S(2)}) collective-permute-start(bf16[64,1024]{1,0:T(8,128)(2,1)S(1)} %slice.155), channel_id=1, source_target_pairs={{0,504},{8,0},{16,8},{24,16},{32,24},{40,32},{48,40},{56,48},{64,5... | collective-permute-start | bytes 393224 | tf_op jit(solution)/shard_map/ppermute | solution.py:16
  107.2 9.1 %collective-permute-start.13 = (bf16[64,1024]{1,0:T(8,128)(2,1)S(1)}, bf16[64,1024]{1,0:T(8,128)(2,1)S(1)}, u32[]{:S(2)}, u32[]{:S(2)}) collective-permute-start(bf16[64,1024]{1,0:T(8,128)(2,1)S(1)} %fusion.19), channel_id=1, source_target_pairs={{0,504},{8,0},{16,8},{24,16},{32,24},{40,32},{48,40},{56,48},{64,5... | collective-permute-start | bytes 393224 | tf_op jit(solution)/shard_map/ppermute | solution.py:16
  111.2 10.0 %collective-permute-start.9 = (bf16[64,1024]{1,0:T(8,128)(2,1)S(1)}, bf16[64,1024]{1,0:T(8,128)(2,1)S(1)}, u32[]{:S(2)}, u32[]{:S(2)}) collective-permute-start(bf16[64,1024]{1,0:T(8,128)(2,1)S(1)} %fusion.23), channel_id=1, source_target_pairs={{0,504},{8,0},{16,8},{24,16},{32,24},{40,32},{48,40},{56,48},{64,5... | collective-permute-start | bytes 393224 | tf_op jit(solution)/shard_map/ppermute | solution.py:16
  116.3 10.0 %collective-permute-start.14 = (bf16[64,1024]{1,0:T(8,128)(2,1)S(1)}, bf16[64,1024]{1,0:T(8,128)(2,1)S(1)}, u32[]{:S(2)}, u32[]{:S(2)}) collective-permute-start(bf16[64,1024]{1,0:T(8,128)(2,1)S(1)} %fusion.18), channel_id=1, source_target_pairs={{0,504},{8,0},{16,8},{24,16},{32,24},{40,32},{48,40},{56,48},{64,5... | collective-permute-start | bytes 393224 | tf_op jit(solution)/shard_map/ppermute | solution.py:16
  121.2 10.0 %collective-permute-start.10 = (bf16[64,1024]{1,0:T(8,128)(2,1)S(1)}, bf16[64,1024]{1,0:T(8,128)(2,1)S(1)}, u32[]{:S(2)}, u32[]{:S(2)}) collective-permute-start(bf16[64,1024]{1,0:T(8,128)(2,1)S(1)} %fusion.22), channel_id=1, source_target_pairs={{0,504},{8,0},{16,8},{24,16},{32,24},{40,32},{48,40},{56,48},{64,5... | collective-permute-start | bytes 393224 | tf_op jit(solution)/shard_map/ppermute | solution.py:16
  126.3 10.6 %collective-permute-start.15 = (bf16[64,1024]{1,0:T(8,128)(2,1)S(1)}, bf16[64,1024]{1,0:T(8,128)(2,1)S(1)}, u32[]{:S(2)}, u32[]{:S(2)}) collective-permute-start(bf16[64,1024]{1,0:T(8,128)(2,1)S(1)} %fusion.17), channel_id=1, source_target_pairs={{0,504},{8,0},{16,8},{24,16},{32,24},{40,32},{48,40},{56,48},{64,5... | collective-permute-start | bytes 393224 | tf_op jit(solution)/shard_map/ppermute | solution.py:16
  131.9 7.9 %collective-permute-start.11 = (bf16[64,1024]{1,0:T(8,128)(2,1)}, bf16[64,1024]{1,0:T(8,128)(2,1)}, u32[]{:S(2)}, u32[]{:S(2)}) collective-permute-start(bf16[64,1024]{1,0:T(8,128)(2,1)} %fusion.21), channel_id=1, source_target_pairs={{0,504},{8,0},{16,8},{24,16},{32,24},{40,32},{48,40},{56,48},{64,5... | collective-permute-start | bytes 393224 | tf_op jit(solution)/shard_map/ppermute | solution.py:16
  139.5 93.8 %reduce-scatter.13.cloned.1.call-start = ((), (), s32[]{:S(2)}) async-start(), calls=%async_computation.6 | async-start | bytes 294912
  141.6 308.0 %reduce-scatter.17.cloned.1.call-start = ((), (), s32[]{:S(2)}) async-start(), calls=%async_computation.8 | async-start | bytes 532480
  (38 other events, 255.4 us)
Sparse Core Ops, SparseCore 0:
  10.1 69.3 all-gather.1
  82.3 52.4 reduce-scatter.10
  139.7 46.8 reduce-scatter.14
  189.2 44.0 reduce-scatter.12
  237.7 211.8 reduce-scatter.16
where the time goes:
time: 459 us; the launch traced here: 458 us
  waiting for transfers between devices  337 us (73%)
  starting transfers between devices  50.4 us (11%)
  local copies, waits for them, and re-layouts  27.3 us (6%)
  matrix products  19.8 us (4%)
  between operations  14.7 us (3%)
  other arithmetic  8.21 us (2%)
    unnamed x8, waiting for transfers between devices  296 us
    ppermute x16, starting transfers between devices, shifted(): return lax.ppermute(value, axis, pairs)  50.2 us
    ppermute x16, waiting for transfers between devices, shifted(): return lax.ppermute(value, axis, pairs)  26.7 us
    unnamed x97, local copies, waits for them, and re-layouts  14.1 us
    all_gather x1, waiting for transfers between devices, local(): full_weight = lax.all_gather(out_weight, 'tgt', axis=0, tiled=True)  14.1 us
  transfers between devices with their start and end apart: 21, of which 12 were waited for; matrix products, arithmetic and copies ran while one was open for 11% of the time, Pallas kernels for 0%

commit v1 on v0

--- a/solution.py
+++ b/solution.py
@@ -64,7 +64,9 @@
 
 
 def local(queries, keys, values, out_weight, out_grad):
-    full_weight = lax.all_gather(out_weight, "tgt", axis=0, tiled=True)
+    full_weight = jnp.concatenate(
+        lax.all_to_all(jnp.stack([out_weight] * lax.axis_size("tgt")), "tgt", 0, 0), axis=0
+    )
     current = (keys, values)
     key_list = [keys]
     value_list = [values]

time: 459 us -> 478 us (1.041)
  waiting for transfers between devices: 337 us -> 294 us
  local copies, waits for them, and re-layouts: 27.3 us -> 59.2 us
  matrix products: 19.8 us -> 38.6 us
  starting transfers between devices: 50.4 us -> 59.3 us
    unnamed x8 -> x7, waiting for transfers between devices: 296 us -> 276 us
    all_gather x1 -> x0, waiting for transfers between devices: 14.1 us -> none  [local(): full_weight = lax.all_gather(out_weight, 'tgt', axis=0, tiled=True)]
    all_to_all x0 -> x1, starting transfers between devices: none -> 9.44 us  [local(): lax.all_to_all(jnp.stack([out_weight] * lax.axis_size('tgt')), 'tgt', 0, 0)]
    ppermute x16, waiting for transfers between devices: 26.7 us -> 18.4 us  [shifted(): return lax.ppermute(value, axis, pairs)]
    dot_general x4, matrix products: 2.3 us -> 9.12 us  [head_block(): jnp.einsum('hrj,rhd->jhd', probs_low, grad_heads, preferred_element_type=...]
    reshape x4, local copies, waits for them, and re-layouts: 1.34 us -> 7.54 us  [head_block(): value_part.reshape(width, group_heads * HD)]
    unnamed x97 -> x95, local copies, waits for them, and re-layouts: 14.1 us -> 18.8 us
  transfers between devices with their start and end apart: 21 -> 21, of which waited for: 12 -> 10; matrix products, arithmetic and copies ran while one was open for 11% -> 21% of each run, Pallas kernels for 0% -> 0%
where the time goes in v1:
time: 478 us; the launch traced here: 476 us
  waiting for transfers between devices  294 us (62%)
  starting transfers between devices  59.3 us (12%)
  local copies, waits for them, and re-layouts  59.2 us (12%)
  matrix products  38.6 us (8%)
  between operations  14.5 us (3%)
  other arithmetic  10.4 us (2%)
    unnamed x7, waiting for transfers between devices  276 us
    ppermute x16, starting transfers between devices, shifted(): return lax.ppermute(value, axis, pairs)  49.8 us
    unnamed x95, local copies, waits for them, and re-layouts  18.8 us
    ppermute x16, waiting for transfers between devices, shifted(): return lax.ppermute(value, axis, pairs)  18.4 us
  transfers between devices with their start and end apart: 21, of which 10 were waited for; matrix products, arithmetic and copies ran while one was open for 21% of the time, Pallas kernels for 0%

profile of v1, /device:TPU:8, one launch (start us, length us, event | category | flops | bytes accessed | tf_op | source)
XLA Modules:
  0.0 476.3 jit_solution(2669578371132946056)
XLA Ops:
  7.2 2.6 stack.2
  9.8 9.4 %all-to-all-start = ((bf16[8,128,1024]{2,1,0:T(8,128)(2,1)}), bf16[8,128,1024]{2,1,0:T(8,128)(2,1)S(1)}, u32[]{:S(2)}, u32[]{:S(2)}) async-start(bf16[8,128,1024]{2,1,0:T(8,128)(2,1)} %stack.2), calls=%async_computation | async-start | bytes 4194304 | tf_op jit(solution)/shard_map/all_to_all | solution.py:68
  19.2 1.9 collective-permute-start
  26.8 4.3 collective-permute-done
  37.4 3.9 collective-permute-done.1
  46.7 4.4 collective-permute-done.2
  57.6 3.4 collective-permute-done.3
  68.2 2.2 fusion.50
  75.8 2.2 fusion.51
  84.3 2.0 convolution_convert_fusion
  114.9 4.0 collective-permute-start.8
  118.9 2.3 fusion.24
  123.1 2.3 fusion.27
  127.3 2.2 fusion.30
  131.4 2.3 fusion.33
  137.1 1.9 collective-permute-start.12
  142.0 7.0 %collective-permute-start.13 = (bf16[64,1024]{1,0:T(8,128)(2,1)S(1)}, bf16[64,1024]{1,0:T(8,128)(2,1)S(1)}, u32[]{:S(2)}, u32[]{:S(2)}) collective-permute-start(bf16[64,1024]{1,0:T(8,128)(2,1)S(1)} %fusion.19), channel_id=1, source_target_pairs={{0,504},{8,0},{16,8},{24,16},{32,24},{40,32},{48,40},{56,48},{64,5... | collective-permute-start | bytes 393224 | tf_op jit(solution)/shard_map/ppermute | solution.py:16
  149.1 2.8 collective-permute-start.10
  151.9 7.0 %collective-permute-start.14 = (bf16[64,1024]{1,0:T(8,128)(2,1)S(1)}, bf16[64,1024]{1,0:T(8,128)(2,1)S(1)}, u32[]{:S(2)}, u32[]{:S(2)}) collective-permute-start(bf16[64,1024]{1,0:T(8,128)(2,1)S(1)} %fusion.18), channel_id=1, source_target_pairs={{0,504},{8,0},{16,8},{24,16},{32,24},{40,32},{48,40},{56,48},{64,5... | collective-permute-start | bytes 393224 | tf_op jit(solution)/shard_map/ppermute | solution.py:16
  159.0 2.8 collective-permute-start.11
  162.5 7.0 %collective-permute-start.15 = (bf16[64,1024]{1,0:T(8,128)(2,1)}, bf16[64,1024]{1,0:T(8,128)(2,1)}, u32[]{:S(2)}, u32[]{:S(2)}) collective-permute-start(bf16[64,1024]{1,0:T(8,128)(2,1)} %fusion.17), channel_id=1, source_target_pairs={{0,504},{8,0},{16,8},{24,16},{32,24},{40,32},{48,40},{56,48},{64,5... | collective-permute-start | bytes 393224 | tf_op jit(solution)/shard_map/ppermute | solution.py:16
  189.5 15.4 %reduce-scatter.13.cloned.1.call-done = bf16[128,64]{1,0:T(8,128)(2,1)} async-done(((bf16[1024,64]{1,0:T(8,128)(2,1)}), bf16[128,64]{1,0:T(8,128)(2,1)}) %reduce-scatter.13.cloned.1.call-update) | async-done | bytes 16400
  206.3 45.5 %reduce-scatter.15.cloned.1.call-done = bf16[128,64]{1,0:T(8,128)(2,1)} async-done(((bf16[1024,64]{1,0:T(8,128)(2,1)}), bf16[128,64]{1,0:T(8,128)(2,1)}) %reduce-scatter.15.cloned.1.call-update) | async-done | bytes 16400
  253.3 214.9 %reduce-scatter.17.cloned.1.call-done = f32[16,128]{1,0:T(8,128)} async-done(((f32[1024,128]{1,0:T(8,128)}), f32[16,128]{1,0:T(8,128)}) %reduce-scatter.17.cloned.1.call-update) | async-done | bytes 8208
  (196 shorter events, 107.8 us)
Async XLA Ops:
  7.2 77.1 %copy-start = (bf16[128,1024]{1,0:T(8,128)(2,1)S(1)}, bf16[128,1024]{1,0:T(8,128)(2,1)}, u32[]{:S(2)}) copy-start(bf16[128,1024]{1,0:T(8,128)(2,1)} %param.9) | copy-start | bytes 786436
  9.8 13.3 %copy-start.29 = (bf16[128,1024]{1,0:T(8,128)(2,1)S(1)}, bf16[128,1024]{1,0:T(8,128)(2,1)}, u32[]{:S(2)}) copy-start(bf16[128,1024]{1,0:T(8,128)(2,1)} %param.5) | copy-start | bytes 786436
  9.8 76.6 %all-to-all-start = ((bf16[8,128,1024]{2,1,0:T(8,128)(2,1)}), bf16[8,128,1024]{2,1,0:T(8,128)(2,1)S(1)}, u32[]{:S(2)}, u32[]{:S(2)}) async-start(bf16[8,128,1024]{2,1,0:T(8,128)(2,1)} %stack.2), calls=%async_computation | async-start | bytes 4194304 | tf_op jit(solution)/shard_map/all_to_all | solution.py:68
  19.2 163.3 %reduce-scatter.11.cloned.1.call-start = ((), (), s32[]{:S(2)}) async-start(), calls=%async_computation.5 | async-start | bytes 2359296 | tf_op jit(solution)/shard_map/reduce_scatter | solution.py:119
  19.2 11.8 %collective-permute-start = (bf16[64,1024]{1,0:T(8,128)(2,1)S(1)}, bf16[64,1024]{1,0:T(8,128)(2,1)}, u32[]{:S(2)}, u32[]{:S(2)}) collective-permute-start(bf16[64,1024]{1,0:T(8,128)(2,1)S(1)} %copy-done.35), channel_id=1, source_target_pairs={{0,8},{8,16},{16,24},{24,32},{32,40},{40,48},{48,56},{56,64},{64,7... | collective-permute-start | bytes 393224 | tf_op jit(solution)/shard_map/ppermute | solution.py:16
  21.2 13.4 %collective-permute-start.4 = (bf16[64,1024]{1,0:T(8,128)(2,1)S(1)}, bf16[64,1024]{1,0:T(8,128)(2,1)}, u32[]{:S(2)}, u32[]{:S(2)}) collective-permute-start(bf16[64,1024]{1,0:T(8,128)(2,1)S(1)} %copy-done.36), channel_id=1, source_target_pairs={{0,8},{8,16},{16,24},{24,32},{32,40},{40,48},{48,56},{56,64},{64,7... | collective-permute-start | bytes 393224 | tf_op jit(solution)/shard_map/ppermute | solution.py:16
  31.1 10.2 %collective-permute-start.1 = (bf16[64,1024]{1,0:T(8,128)(2,1)}, bf16[64,1024]{1,0:T(8,128)(2,1)S(1)}, u32[]{:S(2)}, u32[]{:S(2)}) collective-permute-start(bf16[64,1024]{1,0:T(8,128)(2,1)} %collective-permute-done), channel_id=1, source_target_pairs={{0,8},{8,16},{16,24},{24,32},{32,40},{40,48},{48,56},{56,64},{64,7... | collective-permute-start | bytes 393224 | tf_op jit(solution)/shard_map/ppermute | solution.py:16
  34.6 10.2 %collective-permute-start.5 = (bf16[64,1024]{1,0:T(8,128)(2,1)}, bf16[64,1024]{1,0:T(8,128)(2,1)S(1)}, u32[]{:S(2)}, u32[]{:S(2)}) collective-permute-start(bf16[64,1024]{1,0:T(8,128)(2,1)} %collective-permute-done.4), channel_id=1, source_target_pairs={{0,8},{8,16},{16,24},{24,32},{32,40},{40,48},{48,56},{56,64},{64,7... | collective-permute-start | bytes 393224 | tf_op jit(solution)/shard_map/ppermute | solution.py:16
  41.3 9.9 %collective-permute-start.2 = (bf16[64,1024]{1,0:T(8,128)(2,1)S(1)}, bf16[64,1024]{1,0:T(8,128)(2,1)S(1)}, u32[]{:S(2)}, u32[]{:S(2)}) collective-permute-start(bf16[64,1024]{1,0:T(8,128)(2,1)S(1)} %collective-permute-done.1), channel_id=1, source_target_pairs={{0,8},{8,16},{16,24},{24,32},{32,40},{40,48},{48,56},{56,64},{64,7... | collective-permute-start | bytes 393224 | tf_op jit(solution)/shard_map/ppermute | solution.py:16
  44.8 10.0 %collective-permute-start.6 = (bf16[64,1024]{1,0:T(8,128)(2,1)S(1)}, bf16[64,1024]{1,0:T(8,128)(2,1)}, u32[]{:S(2)}, u32[]{:S(2)}) collective-permute-start(bf16[64,1024]{1,0:T(8,128)(2,1)S(1)} %collective-permute-done.5), channel_id=1, source_target_pairs={{0,8},{8,16},{16,24},{24,32},{32,40},{40,48},{48,56},{56,64},{64,7... | collective-permute-start | bytes 393224 | tf_op jit(solution)/shard_map/ppermute | solution.py:16
  51.2 9.9 %collective-permute-start.3 = (bf16[64,1024]{1,0:T(8,128)(2,1)S(1)}, bf16[64,1024]{1,0:T(8,128)(2,1)S(1)}, u32[]{:S(2)}, u32[]{:S(2)}) collective-permute-start(bf16[64,1024]{1,0:T(8,128)(2,1)S(1)} %collective-permute-done.2), channel_id=1, source_target_pairs={{0,8},{8,16},{16,24},{24,32},{32,40},{40,48},{48,56},{56,64},{64,7... | collective-permute-start | bytes 393224 | tf_op jit(solution)/shard_map/ppermute | solution.py:16
  54.8 10.5 %collective-permute-start.7 = (bf16[64,1024]{1,0:T(8,128)(2,1)}, bf16[64,1024]{1,0:T(8,128)(2,1)}, u32[]{:S(2)}, u32[]{:S(2)}) collective-permute-start(bf16[64,1024]{1,0:T(8,128)(2,1)} %collective-permute-done.6), channel_id=1, source_target_pairs={{0,8},{8,16},{16,24},{24,32},{32,40},{40,48},{48,56},{56,64},{64,7... | collective-permute-start | bytes 393224 | tf_op jit(solution)/shard_map/ppermute | solution.py:16
  86.3 118.6 %reduce-scatter.13.cloned.1.call-start = ((), (), s32[]{:S(2)}) async-start(), calls=%async_computation.6 | async-start | bytes 294912
  114.9 24.1 %collective-permute-start.8 = (bf16[64,1024]{1,0:T(8,128)(2,1)}, bf16[64,1024]{1,0:T(8,128)(2,1)}, u32[]{:S(2)}, u32[]{:S(2)}) collective-permute-start(bf16[64,1024]{1,0:T(8,128)(2,1)} %slice.155), channel_id=1, source_target_pairs={{0,504},{8,0},{16,8},{24,16},{32,24},{40,32},{48,40},{56,48},{64,5... | collective-permute-start | bytes 393224 | tf_op jit(solution)/shard_map/ppermute | solution.py:16
  137.1 24.7 %copy-start.3 = (f32[320,1024]{1,0:T(8,128)}, f32[320,1024]{1,0:T(8,128)S(1)}, u32[]{:S(2)}) copy-start(f32[320,1024]{1,0:T(8,128)S(1)} %pad_maximum_fusion.1) | copy-start | bytes 3932164
  137.1 4.8 %collective-permute-start.12 = (bf16[64,1024]{1,0:T(8,128)(2,1)S(1)}, bf16[64,1024]{1,0:T(8,128)(2,1)S(1)}, u32[]{:S(2)}, u32[]{:S(2)}) collective-permute-start(bf16[64,1024]{1,0:T(8,128)(2,1)S(1)} %slice.154), channel_id=1, source_target_pairs={{0,504},{8,0},{16,8},{24,16},{32,24},{40,32},{48,40},{56,48},{64,5... | collective-permute-start | bytes 393224 | tf_op jit(solution)/shard_map/ppermute | solution.py:16
  140.0 9.0 %collective-permute-start.9 = (bf16[64,1024]{1,0:T(8,128)(2,1)S(1)}, bf16[64,1024]{1,0:T(8,128)(2,1)S(1)}, u32[]{:S(2)}, u32[]{:S(2)}) collective-permute-start(bf16[64,1024]{1,0:T(8,128)(2,1)S(1)} %fusion.23), channel_id=1, source_target_pairs={{0,504},{8,0},{16,8},{24,16},{32,24},{40,32},{48,40},{56,48},{64,5... | collective-permute-start | bytes 393224 | tf_op jit(solution)/shard_map/ppermute | solution.py:16
  142.0 9.9 %collective-permute-start.13 = (bf16[64,1024]{1,0:T(8,128)(2,1)S(1)}, bf16[64,1024]{1,0:T(8,128)(2,1)S(1)}, u32[]{:S(2)}, u32[]{:S(2)}) collective-permute-start(bf16[64,1024]{1,0:T(8,128)(2,1)S(1)} %fusion.19), channel_id=1, source_target_pairs={{0,504},{8,0},{16,8},{24,16},{32,24},{40,32},{48,40},{56,48},{64,5... | collective-permute-start | bytes 393224 | tf_op jit(solution)/shard_map/ppermute | solution.py:16
  149.1 9.9 %collective-permute-start.10 = (bf16[64,1024]{1,0:T(8,128)(2,1)S(1)}, bf16[64,1024]{1,0:T(8,128)(2,1)S(1)}, u32[]{:S(2)}, u32[]{:S(2)}) collective-permute-start(bf16[64,1024]{1,0:T(8,128)(2,1)S(1)} %fusion.22), channel_id=1, source_target_pairs={{0,504},{8,0},{16,8},{24,16},{32,24},{40,32},{48,40},{56,48},{64,5... | collective-permute-start | bytes 393224 | tf_op jit(solution)/shard_map/ppermute | solution.py:16
  151.9 9.9 %collective-permute-start.14 = (bf16[64,1024]{1,0:T(8,128)(2,1)S(1)}, bf16[64,1024]{1,0:T(8,128)(2,1)S(1)}, u32[]{:S(2)}, u32[]{:S(2)}) collective-permute-start(bf16[64,1024]{1,0:T(8,128)(2,1)S(1)} %fusion.18), channel_id=1, source_target_pairs={{0,504},{8,0},{16,8},{24,16},{32,24},{40,32},{48,40},{56,48},{64,5... | collective-permute-start | bytes 393224 | tf_op jit(solution)/shard_map/ppermute | solution.py:16
  159.0 10.5 %collective-permute-start.11 = (bf16[64,1024]{1,0:T(8,128)(2,1)S(1)}, bf16[64,1024]{1,0:T(8,128)(2,1)S(1)}, u32[]{:S(2)}, u32[]{:S(2)}) collective-permute-start(bf16[64,1024]{1,0:T(8,128)(2,1)S(1)} %fusion.21), channel_id=1, source_target_pairs={{0,504},{8,0},{16,8},{24,16},{32,24},{40,32},{48,40},{56,48},{64,5... | collective-permute-start | bytes 393224 | tf_op jit(solution)/shard_map/ppermute | solution.py:16
  162.5 9.8 %collective-permute-start.15 = (bf16[64,1024]{1,0:T(8,128)(2,1)}, bf16[64,1024]{1,0:T(8,128)(2,1)}, u32[]{:S(2)}, u32[]{:S(2)}) collective-permute-start(bf16[64,1024]{1,0:T(8,128)(2,1)} %fusion.17), channel_id=1, source_target_pairs={{0,504},{8,0},{16,8},{24,16},{32,24},{40,32},{48,40},{56,48},{64,5... | collective-permute-start | bytes 393224 | tf_op jit(solution)/shard_map/ppermute | solution.py:16
  172.0 79.9 %reduce-scatter.15.cloned.1.call-start = ((), (), s32[]{:S(2)}) async-start(), calls=%async_computation.7 | async-start | bytes 294912
  175.8 292.5 %reduce-scatter.17.cloned.1.call-start = ((), (), s32[]{:S(2)}) async-start(), calls=%async_computation.8 | async-start | bytes 532480
  (37 other events, 131.1 us)
Sparse Core Ops, SparseCore 0:
  86.4 48.4 reduce-scatter.10
  172.1 32.7 reduce-scatter.12
  207.7 44.1 reduce-scatter.14
  256.3 211.8 reduce-scatter.16
